TPU v7x, 32 devices: a whole 2x2x4 slice. The times are simulated.
32 devices in a mesh: rep: 4 (over y, x), inner: 8 (over z, core).
Axes of the slice: x: 2, y: 2, z: 4, core: 2. Of those that a mesh axis runs over, the one named last changes fastest.
Arguments:
- tokens: bfloat16 [4096, 1024], P(('rep', 'inner')), may hold values from -6 to 6
- cotangent: bfloat16 [4096, 1024], P(('rep', 'inner')), may hold values from -6 to 6
- qkv_weight: bfloat16 [1024, 3072], P('inner'), may hold values from -0.1875 to 0.1875
- out_weight: bfloat16 [1024, 1024], P('inner'), may hold values from -3.5 to 3.5
- in_weight: bfloat16 [1024, 5248], P('inner'), may hold values from -0.1875 to 0.1875
- down_weight: bfloat16 [2624, 1024], P('inner'), may hold values from -0.125 to 0.125
- gain_one: bfloat16 [1024], P('inner'), may hold values from 0.5 to 1.5
- gain_two: bfloat16 [1024], P('inner'), may hold values from 0.5 to 1.5
Outputs:
- layer_out: bfloat16 [4096, 1024], P(('rep', 'inner'))
- input_grad: bfloat16 [4096, 1024], P(('rep', 'inner'))
- qkv_grad: float32 [1024, 3072], P('inner')
- out_grad: float32 [1024, 1024], P('inner')
- in_grad: float32 [1024, 5248], P('inner')
- down_grad: float32 [2624, 1024], P('inner')
- gain_one_grad: float32 [1024], P('inner')
- gain_two_grad: float32 [1024], P('inner')
All inputs are finite; a program needn't handle non-finite values.
Results may differ from a plain program's by a relative error of at most 0.023.
Values may be sent and summed in bfloat16 or wider, within the bound.
No kernel may reach another device: no remote copies, remote signals or barrier semaphores. Data moves between devices by JAX's collectives and lax.ppermute only.
A program may use at most 256 MiB of HBM per device.

v0:
```python
import jax
import jax.numpy as jnp
from jax import lax
from jax.sharding import PartitionSpec as P

HEAD_DIM = 64
EPSILON = 1e-05
THETA = 160000.0


def norm_rows(values, gain_row):
    centred = values - jnp.mean(values, axis=-1, keepdims=True)
    inv_scale = lax.rsqrt(jnp.mean(centred * centred, axis=-1, keepdims=True) + EPSILON)
    return centred * inv_scale * gain_row


def rotate(values, cos_table, sine_table):
    half_width = values.shape[-1] // 2
    first_half = values[..., :half_width]
    second_half = values[..., half_width:]
    return jnp.concatenate(
        [
            first_half * cos_table - second_half * sine_table,
            second_half * cos_table + first_half * sine_table,
        ],
        axis=-1,
    )


def geglu(hidden):
    half_width = hidden.shape[-1] // 2
    return jax.nn.gelu(hidden[:, :half_width], approximate=False) * hidden[:, half_width:]


def contract_rows(left_mat, right_mat):
    return lax.dot_general(
        left_mat, right_mat, (((0,), (0,)), ((), ())), preferred_element_type=jnp.float32
    )


def contract_cols(left_mat, right_mat):
    return lax.dot_general(
        left_mat, right_mat, (((1,), (1,)), ((), ())), preferred_element_type=jnp.float32
    )


def on_device(
    tokens, cotangent, qkv_weight, out_weight, in_weight, down_weight, gain_one, gain_two
):
    row_count = tokens.shape[0]
    model_width = tokens.shape[1]
    head_count = model_width // HEAD_DIM
    score_scale = HEAD_DIM ** (-0.5)
    gathered = (
        lax.all_gather(qkv_weight, "inner", axis=0, tiled=True),
        lax.all_gather(out_weight, "inner", axis=0, tiled=True),
        lax.all_gather(in_weight, "inner", axis=0, tiled=True),
        lax.all_gather(down_weight, "inner", axis=0, tiled=True),
        lax.all_gather(gain_one, "inner", axis=0, tiled=True),
        lax.all_gather(gain_two, "inner", axis=0, tiled=True),
    )
    w_qkv, w_out, w_in, w_down, first_gain, second_gain = gathered
    tok_place = (
        lax.axis_index("inner") * row_count + jnp.arange(row_count, dtype=jnp.int32)
    ).astype(jnp.float32)
    inv_freq = 1.0 / THETA ** (jnp.arange(HEAD_DIM // 2, dtype=jnp.float32) * (2.0 / HEAD_DIM))
    tok_angle = tok_place[:, None] * inv_freq[None, :]
    cos_table = jnp.cos(tok_angle)[:, None, :]
    sine_table = jnp.sin(tok_angle)[:, None, :]

    def split_heads(projected):
        query_part = rotate(
            projected[:, :model_width].reshape(row_count, head_count, HEAD_DIM),
            cos_table,
            sine_table,
        )
        key_part = rotate(
            projected[:, model_width : 2 * model_width].reshape(row_count, head_count, HEAD_DIM),
            cos_table,
            sine_table,
        )
        value_part = projected[:, 2 * model_width :].reshape(row_count, head_count, HEAD_DIM)
        return (query_part, key_part, value_part)

    inputs = tokens.astype(jnp.float32)
    gain_first = first_gain.astype(jnp.float32)
    gain_second = second_gain.astype(jnp.float32)
    normed_one = norm_rows(inputs, gain_first).astype(jnp.bfloat16)
    projected = jnp.dot(normed_one, w_qkv, preferred_element_type=jnp.float32)
    query_part, key_part, value_part = split_heads(projected)
    query_heads = query_part.astype(jnp.bfloat16)
    key_flat = key_part.reshape(row_count, model_width).astype(jnp.bfloat16)
    value_flat = value_part.reshape(row_count, model_width).astype(jnp.bfloat16)
    all_keys, all_values = (
        lax.all_gather(key_flat, "inner", axis=0, tiled=True),
        lax.all_gather(value_flat, "inner", axis=0, tiled=True),
    )
    key_count = all_keys.shape[0]
    block_count = max(1, key_count // 512)
    block_rows = key_count // block_count

    def split_blocks(flat):
        return flat.reshape(block_count, block_rows, head_count, HEAD_DIM)

    def scores_of(key_block):
        return (
            jnp.einsum("qhd,khd->hqk", query_heads, key_block, preferred_element_type=jnp.float32)
            * score_scale
        )

    def stats_step(stat_carry, key_block):
        row_top, row_mass = stat_carry
        scores = scores_of(key_block)
        new_top = jnp.maximum(row_top, jnp.max(scores, axis=-1))
        row_mass = row_mass * jnp.exp(row_top - new_top) + jnp.sum(
            jnp.exp(scores - new_top[..., None]), axis=-1
        )
        return ((new_top, row_mass), None)

    start_top = jnp.full((head_count, row_count), -jnp.inf, jnp.float32)
    start_mass = jnp.zeros((head_count, row_count), jnp.float32)
    stat_final, unused_out = lax.scan(stats_step, (start_top, start_mass), split_blocks(all_keys))
    log_mass = stat_final[0] + jnp.log(stat_final[1])

    def mix_step(total_mix, blocks_pair):
        key_block, value_block = blocks_pair
        weights = jnp.exp(scores_of(key_block) - log_mass[..., None]).astype(jnp.bfloat16)
        return (
            total_mix
            + jnp.einsum("hqk,khd->qhd", weights, value_block, preferred_element_type=jnp.float32),
            None,
        )

    start_mix = jnp.zeros((row_count, head_count, HEAD_DIM), jnp.float32)
    mixed_heads, unused_mix = lax.scan(
        mix_step, start_mix, (split_blocks(all_keys), split_blocks(all_values))
    )
    attended = mixed_heads.reshape(row_count, model_width).astype(jnp.bfloat16)
    middle = inputs + jnp.dot(attended, w_out, preferred_element_type=jnp.float32)
    normed_two = norm_rows(middle, gain_second).astype(jnp.bfloat16)
    hidden = jnp.dot(normed_two, w_in, preferred_element_type=jnp.float32)
    gated = geglu(hidden).astype(jnp.bfloat16)
    layer_out = middle + jnp.dot(gated, w_down, preferred_element_type=jnp.float32)
    again = (
        lax.all_gather(qkv_weight, "inner", axis=0, tiled=True),
        lax.all_gather(out_weight, "inner", axis=0, tiled=True),
        lax.all_gather(in_weight, "inner", axis=0, tiled=True),
        lax.all_gather(down_weight, "inner", axis=0, tiled=True),
        lax.all_gather(gain_one, "inner", axis=0, tiled=True),
        lax.all_gather(gain_two, "inner", axis=0, tiled=True),
    )
    w_qkv, w_out, w_in, w_down, first_gain, second_gain = again
    gain_first = first_gain.astype(jnp.float32)
    gain_second = second_gain.astype(jnp.float32)
    grad_down = contract_rows(gated, cotangent)
    grad_gated = contract_cols(cotangent, w_down)
    gate_value, pull_gate = jax.vjp(geglu, hidden)
    grad_hidden = pull_gate(grad_gated)[0].astype(jnp.bfloat16)
    grad_in = contract_rows(normed_two, grad_hidden)
    grad_normed_two = contract_cols(grad_hidden, w_in)
    norm_value, pull_two = jax.vjp(norm_rows, middle, gain_second)
    back_middle, grad_gain_two = pull_two(grad_normed_two)
    grad_middle = cotangent.astype(jnp.float32) + back_middle
    grad_branch = grad_middle.astype(jnp.bfloat16)
    grad_wout = contract_rows(attended, grad_branch)
    grad_attended = contract_cols(grad_branch, w_out).astype(jnp.bfloat16)
    grad_heads = grad_attended.reshape(row_count, head_count, HEAD_DIM)
    offset = jnp.sum(
        grad_heads.astype(jnp.float32)
        * attended.reshape(row_count, head_count, HEAD_DIM).astype(jnp.float32),
        axis=-1,
    ).T
    all_keys, all_values = (
        lax.all_gather(key_flat, "inner", axis=0, tiled=True),
        lax.all_gather(value_flat, "inner", axis=0, tiled=True),
    )

    def score_grads(key_block, value_block):
        soft_probs = jnp.exp(scores_of(key_block) - log_mass[..., None])
        grad_probs = jnp.einsum(
            "qhd,khd->hqk", grad_heads, value_block, preferred_element_type=jnp.float32
        )
        grad_scores = (soft_probs * (grad_probs - offset[..., None])).astype(jnp.bfloat16)
        return (soft_probs, grad_scores)

    def back_step(grad_query, blocks_pair):
        key_block, value_block = blocks_pair
        soft_probs, grad_scores = score_grads(key_block, value_block)
        grad_value = jnp.einsum(
            "hqk,qhd->khd",
            soft_probs.astype(jnp.bfloat16),
            grad_heads,
            preferred_element_type=jnp.float32,
        )
        grad_key = (
            jnp.einsum("hqk,qhd->khd", grad_scores, query_heads, preferred_element_type=jnp.float32)
            * score_scale
        )
        grad_query = (
            grad_query
            + jnp.einsum("hqk,khd->qhd", grad_scores, key_block, preferred_element_type=jnp.float32)
            * score_scale
        )
        return (grad_query, (grad_key, grad_value))

    start_query = jnp.zeros((row_count, head_count, HEAD_DIM), jnp.float32)
    grad_query, key_parts = lax.scan(
        back_step, start_query, (split_blocks(all_keys), split_blocks(all_values))
    )
    own_keys, own_values = (
        lax.psum_scatter(
            key_parts[0].reshape(key_count, model_width).astype(jnp.bfloat16),
            "inner",
            scatter_dimension=0,
            tiled=True,
        ).astype(jnp.float32),
        lax.psum_scatter(
            key_parts[1].reshape(key_count, model_width).astype(jnp.bfloat16),
            "inner",
            scatter_dimension=0,
            tiled=True,
        ).astype(jnp.float32),
    )
    split_value, pull_split = jax.vjp(split_heads, projected)
    grad_projected = pull_split(
        (
            grad_query,
            own_keys.reshape(row_count, head_count, HEAD_DIM),
            own_values.reshape(row_count, head_count, HEAD_DIM),
        )
    )[0].astype(jnp.bfloat16)
    grad_qkv = contract_rows(normed_one, grad_projected)
    grad_normed_one = contract_cols(grad_projected, w_qkv)
    first_value, pull_one = jax.vjp(norm_rows, inputs, gain_first)
    back_inputs, grad_gain_one = pull_one(grad_normed_one)
    input_grad = (grad_middle + back_inputs).astype(jnp.bfloat16)
    summed = (
        lax.psum_scatter(
            grad_qkv.astype(jnp.bfloat16), "inner", scatter_dimension=0, tiled=True
        ).astype(jnp.float32),
        lax.psum_scatter(
            grad_wout.astype(jnp.bfloat16), "inner", scatter_dimension=0, tiled=True
        ).astype(jnp.float32),
        lax.psum_scatter(
            grad_in.astype(jnp.bfloat16), "inner", scatter_dimension=0, tiled=True
        ).astype(jnp.float32),
        lax.psum_scatter(
            grad_down.astype(jnp.bfloat16), "inner", scatter_dimension=0, tiled=True
        ).astype(jnp.float32),
        lax.psum_scatter(
            grad_gain_one.astype(jnp.bfloat16), "inner", scatter_dimension=0, tiled=True
        ).astype(jnp.float32),
        lax.psum_scatter(
            grad_gain_two.astype(jnp.bfloat16), "inner", scatter_dimension=0, tiled=True
        ).astype(jnp.float32),
    )
    summed = (
        lax.psum(summed[0].astype(jnp.bfloat16), "rep").astype(jnp.float32),
        lax.psum(summed[1].astype(jnp.bfloat16), "rep").astype(jnp.float32),
        lax.psum(summed[2].astype(jnp.bfloat16), "rep").astype(jnp.float32),
        lax.psum(summed[3].astype(jnp.bfloat16), "rep").astype(jnp.float32),
        lax.psum(summed[4].astype(jnp.bfloat16), "rep").astype(jnp.float32),
        lax.psum(summed[5].astype(jnp.bfloat16), "rep").astype(jnp.float32),
    )
    return (
        layer_out.astype(jnp.bfloat16),
        input_grad,
        summed[0],
        summed[1],
        summed[2],
        summed[3],
        summed[4],
        summed[5],
    )


def solution(mesh):
    return jax.shard_map(
        on_device,
        mesh=mesh,
        in_specs=(
            P(("rep", "inner"), None),
            P(("rep", "inner"), None),
            P("inner", None),
            P("inner", None),
            P("inner", None),
            P("inner", None),
            P("inner"),
            P("inner"),
        ),
        out_specs=(
            P(("rep", "inner"), None),
            P(("rep", "inner"), None),
            P("inner", None),
            P("inner", None),
            P("inner", None),
            P("inner", None),
            P("inner"),
            P("inner"),
        ),
        check_vma=False,
    )
```

profile of v0, /device:TPU:0, one launch (start us, length us, event | category | flops | bytes accessed | tf_op | source)
XLA Modules:
  0.0 841.6 jit_solution(2752431351207426690)
XLA Ops:
  8.0 13.5 %all-gather = bf16[8,1,128]{2,1,0:T(2,128)(2,1)S(1)} all-gather(bf16[1,1,128]{2,1,0:T(2,128)(2,1)} %bitcast.152), channel_id=1, replica_groups=mesh['rep'=4,'inner'=8] {'inner'}, dimensions={0}, use_global_device_ids=true | all-gather | bytes 2304 | tf_op jit(solution)/shard_map/all_gather | solution.py:59
  22.6 1.2 fusion.55
  24.0 53.2 %all-gather.9.cloned.1.call-done = bf16[1024,3072]{1,0:T(8,128)(2,1)} async-done(((bf16[128,3072]{1,0:T(8,128)(2,1)}), bf16[1024,3072]{1,0:T(8,128)(2,1)}) %all-gather.9.cloned.1.call-update) | async-done | bytes 6291472 | tf_op jit(solution)/shard_map/all_gather | solution.py:55
  77.1 3.9 fusion.70
  85.1 9.2 %all-gather.1 = bf16[8,1,128]{2,1,0:T(2,128)(2,1)S(1)} all-gather(bf16[1,1,128]{2,1,0:T(2,128)(2,1)S(1)} %bitcast.153), channel_id=1, replica_groups=mesh['rep'=4,'inner'=8] {'inner'}, dimensions={0}, use_global_device_ids=true | all-gather | bytes 2304 | tf_op jit(solution)/shard_map/all_gather | solution.py:60
  94.3 17.8 %all-gather.13.cloned.1.call-done = bf16[1024,1024]{0,1:T(8,128)(2,1)} async-done(((bf16[128,1024]{0,1:T(8,128)(2,1)}), bf16[1024,1024]{0,1:T(8,128)(2,1)}) %all-gather.13.cloned.1.call-update) | async-done | bytes 2097168 | tf_op jit(solution)/shard_map/all_gather | solution.py:95
  112.1 4.5 reshape.175
  116.6 2.0 copy.47
  118.6 23.9 %all-gather.11.cloned.1.call-done = bf16[1024,1024]{1,0:T(8,128)(2,1)} async-done(((bf16[128,1024]{1,0:T(8,128)(2,1)}), bf16[1024,1024]{1,0:T(8,128)(2,1)}) %all-gather.11.cloned.1.call-update) | async-done | bytes 2097168 | tf_op jit(solution)/shard_map/all_gather | solution.py:96
  142.5 6.4 reshape.196
  148.8 5.5 copy.46
  154.4 11.6 %while.39 = (s32[]{:T(128)}, f32[16,128]{1,0:T(8,128)S(1)}, f32[16,128]{1,0:T(8,128)S(1)}, bf16[2,512,16,64]{1,3,2,0:T(8,128)(2,1)S(1)}, bf16[128,16,64]{0,2,1:T(8,128)(2,1)S(1)}, /*index=5*/s32[]{:T(128)}, s32[]{:T(128)}) while((s32[]{:T(128)}, f32[16,128]{1,0:T(8,128)S(1)}, f32[16,128]{1,0:T(8,128)S(1)}, ...), condition=%wide.region_5.6_spmd.clone, body=%wide.region_2.5_spmd.clone.sunk | while | flops 139470848 | bytes 9805916 | solution.py:122
  154.4 2.8 bitcast_reduce_fusion.2
  157.2 2.9 fusion.122
  160.1 2.8 bitcast_reduce_fusion.2
  163.0 2.9 fusion.122
  165.9 6.0 while.40
  166.0 2.7 fusion.127
  168.7 2.7 fusion.127
  172.7 2.1 fusion.77
  175.1 100.1 %all-gather.17.cloned.1.call-done = bf16[1024,5248]{1,0:T(8,128)(2,1)} async-done(((bf16[128,5248]{1,0:T(8,128)(2,1)}), bf16[1024,5248]{1,0:T(8,128)(2,1)}) %all-gather.17.cloned.1.call-update) | async-done | bytes 10747920 | tf_op jit(solution)/shard_map/all_gather | solution.py:57
  275.1 7.3 fusion.73
  282.4 49.7 %all-gather.19.cloned.1.call-done = bf16[2624,1024]{1,0:T(8,128)(2,1)} async-done(((bf16[328,1024]{1,0:T(8,128)(2,1)}), bf16[2624,1024]{1,0:T(8,128)(2,1)}) %all-gather.19.cloned.1.call-update) | async-done | bytes 5373968 | tf_op jit(solution)/shard_map/all_gather | solution.py:58
  332.1 7.0 fusion.57
  339.2 1.7 multiply_add_fusion
  340.8 4.4 multiply_reduce_fusion
  345.2 1.4 fusion.74
  348.3 1.5 convolution_convert_fusion.4
  351.0 1.1 multiply_reduce_fusion.1
  352.1 21.2 %while.41 = (s32[]{:T(128)}, f32[128,16,64]{0,2,1:T(8,128)}, bf16[2,512,16,64]{1,3,2,0:T(8,128)(2,1)}, bf16[2,512,16,64]{1,3,2,0:T(8,128)(2,1)}, bf16[2,512,16,6...) while((s32[]{:T(128)}, f32[128,16,64]{0,2,1:T(8,128)}, ...), condition=%wide.region_14.15_spmd.clone, body=%wide.region_13.14_spmd.clone.sunk | while | flops 680394752 | bytes 87058192 | solution.py:207
  353.6 1.2 copy-done.5
  354.8 1.4 multiply_convert_fusion.6
  356.2 1.9 bitcast_dynamic-update-slice_fusion.4
  358.1 2.7 fusion.139
  360.8 1.9 bitcast_dynamic-update-slice_fusion.5
  364.1 1.2 copy-done.5
  365.2 1.4 multiply_convert_fusion.6
  366.7 1.8 bitcast_dynamic-update-slice_fusion.4
  368.5 2.8 fusion.139
  371.3 2.0 bitcast_dynamic-update-slice_fusion.5
  373.3 6.2 copy.63
  379.5 6.5 reshape.192
  386.1 1.5 copy-done.22
  387.6 4.8 copy.62
  392.3 6.5 reshape.190
  399.9 2.0 convolution_convert_fusion.3
  403.1 3.9 convolution_convert_fusion.1
  407.3 13.4 %reduce-scatter.21.cloned.1.call-done = bf16[128,1024]{1,0:T(8,128)(2,1)} async-done(((bf16[1024,1024]{1,0:T(8,128)(2,1)}), bf16[128,1024]{1,0:T(8,128)(2,1)}) %reduce-scatter.21.cloned.1.call-update) | async-done | bytes 262160
  421.9 35.8 %reduce-scatter.19.cloned.1.call-done = bf16[128,1024]{1,0:T(8,128)(2,1)} async-done(((bf16[1024,1024]{1,0:T(8,128)(2,1)}), bf16[128,1024]{1,0:T(8,128)(2,1)}) %reduce-scatter.19.cloned.1.call-update) | async-done | bytes 262160
  459.1 4.6 convolution_convert_fusion.2
  463.8 1.4 copy-done.9
  465.1 7.3 convolution_convert_fusion
  472.5 21.9 %reduce-scatter.13.cloned.1.call-done = bf16[128,1024]{1,0:T(8,128)(2,1)} async-done(((bf16[1024,1024]{1,0:T(8,128)(2,1)}), bf16[128,1024]{1,0:T(8,128)(2,1)}) %reduce-scatter.13.cloned.1.call-update) | async-done | bytes 262160 | tf_op jit(solution)/shard_map/reduce_scatter | solution.py:241
  494.3 62.0 %reduce-scatter.17.cloned.1.call-done = bf16[328,1024]{1,0:T(8,128)(2,1)} async-done(((bf16[2624,1024]{1,0:T(8,128)(2,1)}), bf16[328,1024]{1,0:T(8,128)(2,1)}) %reduce-scatter.17.cloned.1.call-update) | async-done | bytes 671760 | tf_op jit(solution)/shard_map/reduce_scatter | solution.py:247
  556.3 70.6 %reduce-scatter.11.cloned.1.call-done = bf16[128,3072]{1,0:T(8,128)(2,1)} async-done(((bf16[1024,3072]{1,0:T(8,128)(2,1)}), bf16[128,3072]{1,0:T(8,128)(2,1)}) %reduce-scatter.11.cloned.1.call-update) | async-done | bytes 786448 | tf_op jit(solution)/shard_map/reduce_scatter | solution.py:238
  627.0 112.6 %reduce-scatter.15.cloned.1.call-done = bf16[128,5248]{1,0:T(8,128)(2,1)} async-done(((bf16[1024,5248]{1,0:T(8,128)(2,1)}), bf16[128,5248]{1,0:T(8,128)(2,1)}) %reduce-scatter.15.cloned.1.call-update) | async-done | bytes 1343504 | tf_op jit(solution)/shard_map/reduce_scatter | solution.py:244
  740.8 4.2 fusion.46
  745.1 5.7 fusion.56
  751.2 13.6 %all-reduce.11 = (bf16[1024]{0:T(1024)(128)(2,1)S(1)}, bf16[1024]{0:T(1024)(128)(2,1)S(1)}) all-reduce(bf16[1024]{0:T(1024)(128)(2,1)S(1)} %get-tuple-element.260, bf16[1024]{0:T(1024)(128)(2,1)S(1)} %get-tuple-element.258), channel_id=8, replica_groups=mesh['rep'=4,'inner'=8] {'inner'}, use_global_device_ids=true, to_apply=%region_28.29.clone | all-reduce | flops 2048 | bytes 8192
  764.9 9.5 %all-reduce.12 = (bf16[128]{0:T(256)(128)(2,1)S(1)}, bf16[128]{0:T(256)(128)(2,1)S(1)}) all-reduce(bf16[128]{0:T(256)(128)(2,1)S(1)} %dynamic-slice.1, bf16[128]{0:T(256)(128)(2,1)S(1)} %dynamic-slice.3), channel_id=1, replica_groups=mesh['rep'=4,'inner'=8] {'rep'}, use_global_device_ids=true, to_apply=%region_29.30 | all-reduce | flops 256 | bytes 1024 | tf_op jit(solution)/shard_map/psum | solution.py:262
  776.4 52.0 %all-reduce.16.cloned.1.call-done = (bf16[128,3072]{1,0:T(8,128)(2,1)}, bf16[128,1024]{1,0:T(8,128)(2,1)}, bf16[128,5248]{1,0:T(8,128)(2,1)}, bf16[328,1024]{1,0:T(8,128)(2,1)}) async-done(((bf16[128,3072]{1,0:T(8,128)(2,1)}, bf16[128,1024]{1,0:T(8,128)(2,1)}, bf16[128,5248]{1,0:T(8,128)(2,1)}, bf16[328,1024]{1,0:T(8,128)(2,1)}), (bf16[128,3072]{1,0:T(8,128)(2,1)}, bf16[128,1024]{1,0:T(8,128)(2,1)}, ...) | async-done | bytes 3063824 | tf_op jit(solution)/shard_map/psum | solution.py:258
  828.4 3.1 convert_element_type.166
  831.5 1.3 convert_element_type.162
  832.8 1.2 convert_element_type.168
  (152 shorter events, 21.6 us)
Async XLA Ops:
  7.2 70.0 %copy-start.7 = (bf16[128,1024]{1,0:T(8,128)(2,1)S(1)}, bf16[128,1024]{1,0:T(8,128)(2,1)}, u32[]{:S(2)}) copy-start(bf16[128,1024]{1,0:T(8,128)(2,1)} %param.14) | copy-start | bytes 786436
  7.2 70.0 %all-gather.9.cloned.1.call-start = ((), (), s32[]{:S(2)}) async-start(), calls=%async_computation.6 | async-start | bytes 7077888 | tf_op jit(solution)/shard_map/all_gather | solution.py:55
  7.9 104.2 %all-gather.13.cloned.1.call-start = ((), (), s32[]{:S(2)}) async-start(), calls=%async_computation.8 | async-start | bytes 2359296 | tf_op jit(solution)/shard_map/all_gather | solution.py:95
  82.4 2.7 copy-start.31
  82.4 60.0 %all-gather.11.cloned.1.call-start = ((), (), s32[]{:S(2)}) async-start(), calls=%async_computation.7 | async-start | bytes 2359296 | tf_op jit(solution)/shard_map/all_gather | solution.py:96
  83.3 89.3 %all-gather.15.cloned.1.call-start = ((), (), s32[]{:S(2)}) async-start(), calls=%async_computation.9 | async-start | bytes 2359296 | tf_op jit(solution)/shard_map/all_gather | solution.py:56
  83.8 191.3 %all-gather.17.cloned.1.call-start = ((), (), s32[]{:S(2)}) async-start(), calls=%async_computation.10 | async-start | bytes 12091392 | tf_op jit(solution)/shard_map/all_gather | solution.py:57
  84.4 247.7 %all-gather.19.cloned.1.call-start = ((), (), s32[]{:S(2)}) async-start(), calls=%async_computation.11 | async-start | bytes 6045696 | tf_op jit(solution)/shard_map/all_gather | solution.py:58
  85.0 335.7 %reduce-scatter.21.cloned.1.call-start = ((), (), s32[]{:S(2)}) async-start(), calls=%async_computation.17 | async-start | bytes 2359296
  171.9 0.8 copy-start.23
  172.0 2.9 copy-start.20
  275.1 57.0 %copy-start.16 = (bf16[128,1024]{1,0:T(8,128)(2,1)S(1)}, bf16[128,1024]{1,0:T(8,128)(2,1)}, u32[]{:S(2)}) copy-start(bf16[128,1024]{1,0:T(8,128)(2,1)} %param.15) | copy-start | bytes 786436
  332.1 7.0 copy-start.10
  332.1 8.7 %copy-start.4 = (bf16[1024,5248]{1,0:T(8,128)(2,1)S(1)}, bf16[1024,5248]{1,0:T(8,128)(2,1)}, u32[]{:S(2)}) copy-start(bf16[1024,5248]{1,0:T(8,128)(2,1)} %all-gather.17.cloned.1.call-done) | copy-start | bytes 32243716
  339.1 1.7 copy-start.13
  340.8 4.4 copy-start.8
  345.2 3.1 copy-start.12
  346.7 0.8 copy-start.14
  347.6 0.7 copy-start.18
  352.3 1.3 copy-start.2
  352.3 2.5 copy-start.5
  353.6 2.6 copy-start
  358.1 2.7 copy-start.1
  360.8 1.9 copy-start.3
  362.7 1.3 copy-start.2
  362.7 2.5 copy-start.5
  364.1 2.6 copy-start
  368.5 2.8 copy-start.1
  371.3 2.0 copy-start.3
  386.0 1.6 copy-start.22
  386.0 71.6 %reduce-scatter.19.cloned.1.call-start = ((), (), s32[]{:S(2)}) async-start(), calls=%async_computation.16 | async-start | bytes 2359296
  398.9 1.0 copy-start.19
  398.9 1.0 copy-start.21
  398.9 95.4 %reduce-scatter.13.cloned.1.call-start = ((), (), s32[]{:S(2)}) async-start(), calls=%async_computation.13 | async-start | bytes 2359296 | tf_op jit(solution)/shard_map/reduce_scatter | solution.py:241
  401.9 1.1 copy-start.11
  401.9 1.2 copy-start.17
  402.0 154.4 %reduce-scatter.17.cloned.1.call-start = ((), (), s32[]{:S(2)}) async-start(), calls=%async_computation.15 | async-start | bytes 6045696 | tf_op jit(solution)/shard_map/reduce_scatter | solution.py:247
  407.0 51.8 %copy-start.6 = (f32[128,16,64]{0,2,1:T(8,128)S(1)}, f32[128,16,64]{0,2,1:T(8,128)}, u32[]{:S(2)}) copy-start(f32[128,16,64]{0,2,1:T(8,128)} %get-tuple-element.127) | copy-start | bytes 1572868
  407.0 219.9 %reduce-scatter.11.cloned.1.call-start = ((), (), s32[]{:S(2)}) async-start(), calls=%async_computation.12 | async-start | bytes 7077888 | tf_op jit(solution)/shard_map/reduce_scatter | solution.py:238
  459.0 4.6 copy-start.24
  459.1 4.6 copy-start.26
  463.7 1.4 copy-start.9
  463.7 275.8 %reduce-scatter.15.cloned.1.call-start = ((), (), s32[]{:S(2)}) async-start(), calls=%async_computation.14 | async-start | bytes 12091392 | tf_op jit(solution)/shard_map/reduce_scatter | solution.py:244
  472.4 267.2 %copy-start.32 = (u32[32]{0:T(128)S(1)}, u32[32]{0:T(128)}, u32[]{:S(2)}) copy-start(u32[32]{0:T(128)} %constant.153) | copy-start | bytes 388
  472.4 356.0 %all-reduce.16.cloned.1.call-start = ((), (), s32[]{:S(2)}) async-start(), calls=%async_computation.18 | async-start | bytes 6127616 | tf_op jit(solution)/shard_map/psum | solution.py:258
  740.8 4.3 copy-start.25
  740.8 4.3 copy-start.27
  745.1 30.3 %copy-start.15 = (f32[128,1024]{1,0:T(8,128)S(1)}, f32[128,1024]{1,0:T(8,128)}, u32[]{:S(2)}) copy-start(f32[128,1024]{1,0:T(8,128)} %copy-done.14) | copy-start | bytes 1572868
  828.4 3.1 copy-start.28
  831.5 1.3 copy-start.29
  832.8 1.2 copy-start.30
Sparse Core Ops, SparseCore 0:
  9.7 67.4 all-gather.8
  82.5 29.4 all-gather.12
  114.3 28.1 all-gather.10
  143.9 28.5 all-gather.14
  174.0 101.0 all-gather.16
  276.6 55.4 all-gather.18
  386.1 34.5 reduce-scatter.20
  423.0 34.6 reduce-scatter.18
  460.0 34.3 reduce-scatter.12
  496.5 59.8 reduce-scatter.16
  558.7 68.1 reduce-scatter.10
  629.2 110.2 reduce-scatter.14
  743.5 84.9 all-reduce.15
where the time goes:
time: 849 us; the launch traced here: 842 us
  waiting for transfers between devices  616 us (73%)
  matrix products  82.5 us (10%)
  local copies, waits for them, and re-layouts  57.8 us (7%)
  blocking collectives  45.8 us (5%)
  other arithmetic  23 us (3%)
  between operations  15.2 us (2%)
    reduce_scatter x1, waiting for transfers between devices, on_device(): lax.psum_scatter(grad_in.astype(jnp.bfloat16), 'inner', scatter_dimension...  113 us
    all_gather x1, waiting for transfers between devices, on_device(): lax.all_gather(in_weight, 'inner', axis=0, tiled=True)  100 us
    reduce_scatter x1, waiting for transfers between devices, on_device(): lax.psum_scatter(grad_qkv.astype(jnp.bfloat16), 'inner', scatter_dimensio...  70.6 us
    reduce_scatter x1, waiting for transfers between devices, on_device(): lax.psum_scatter(grad_down.astype(jnp.bfloat16), 'inner', scatter_dimensi...  62 us
    all_gather x1, waiting for transfers between devices, on_device(): lax.all_gather(qkv_weight, 'inner', axis=0, tiled=True)  53.2 us
    psum x1, waiting for transfers between devices, on_device(): lax.psum(summed[0].astype(jnp.bfloat16), 'rep').astype(jnp.float32)  52 us
    unnamed x15, waiting for transfers between devices  51.6 us
    all_gather x1, waiting for transfers between devices, on_device(): lax.all_gather(down_weight, 'inner', axis=0, tiled=True)  49.7 us
  transfers between devices with their start and end apart: 13, of which 13 were waited for; matrix products, arithmetic and copies ran while one was open for 11% of the time, Pallas kernels for 0%

commit v1 on v0

--- a/solution.py
+++ b/solution.py
@@ -255,7 +255,7 @@
         ).astype(jnp.float32),
     )
     summed = (
-        lax.psum(summed[0].astype(jnp.bfloat16), "rep").astype(jnp.float32),
+        jnp.sum(lax.all_gather(summed[0].astype(jnp.bfloat16), "rep"), axis=0).astype(jnp.float32),
         lax.psum(summed[1].astype(jnp.bfloat16), "rep").astype(jnp.float32),
         lax.psum(summed[2].astype(jnp.bfloat16), "rep").astype(jnp.float32),
         lax.psum(summed[3].astype(jnp.bfloat16), "rep").astype(jnp.float32),

time: 849 us -> 884 us (1.041)
  waiting for transfers between devices: 616 us -> 648 us
    psum x1, waiting for transfers between devices: 52 us -> 72.8 us  [on_device(): lax.psum(summed[1].astype(jnp.bfloat16), 'rep').astype(jnp.float32)]
    reduce_scatter x1, waiting for transfers between devices: 70.6 us -> 51.8 us  [on_device(): lax.psum_scatter(grad_qkv.astype(jnp.bfloat16), 'inner', scatter_dimensio...]
    reduce_scatter x1, waiting for transfers between devices: 21.9 us -> 36.8 us  [on_device(): lax.psum_scatter(grad_wout.astype(jnp.bfloat16), 'inner', scatter_dimensi...]
    unnamed x15 -> x16, waiting for transfers between devices: 51.6 us -> 59.6 us
    unnamed x67 -> x65, local copies, waits for them, and re-layouts: 41.2 us -> 40.8 us
  transfers between devices with their start and end apart: 13 -> 14, of which waited for: 13 -> 14; matrix products, arithmetic and copies ran while one was open for 11% -> 10% of each run, Pallas kernels for 0% -> 0%
where the time goes in v1:
time: 884 us; the launch traced here: 877 us
  waiting for transfers between devices  648 us (73%)
  matrix products  82.5 us (9%)
  local copies, waits for them, and re-layouts  57.5 us (7%)
  blocking collectives  46.3 us (5%)
  other arithmetic  25.5 us (3%)
  between operations  15.2 us (2%)
    reduce_scatter x1, waiting for transfers between devices, on_device(): lax.psum_scatter(grad_in.astype(jnp.bfloat16), 'inner', scatter_dimension...  113 us
    all_gather x1, waiting for transfers between devices, on_device(): lax.all_gather(in_weight, 'inner', axis=0, tiled=True)  100 us
    psum x1, waiting for transfers between devices, on_device(): lax.psum(summed[1].astype(jnp.bfloat16), 'rep').astype(jnp.float32)  72.8 us
    reduce_scatter x1, waiting for transfers between devices, on_device(): lax.psum_scatter(grad_down.astype(jnp.bfloat16), 'inner', scatter_dimensi...  62.1 us
    unnamed x16, waiting for transfers between devices  59.6 us
    all_gather x1, waiting for transfers between devices, on_device(): lax.all_gather(qkv_weight, 'inner', axis=0, tiled=True)  53.2 us
    reduce_scatter x1, waiting for transfers between devices, on_device(): lax.psum_scatter(grad_qkv.astype(jnp.bfloat16), 'inner', scatter_dimensio...  51.8 us
    all_gather x1, waiting for transfers between devices, on_device(): lax.all_gather(down_weight, 'inner', axis=0, tiled=True)  49.7 us
  transfers between devices with their start and end apart: 14, of which 14 were waited for; matrix products, arithmetic and copies ran while one was open for 10% of the time, Pallas kernels for 0%

profile of v1, /device:TPU:0, one launch (start us, length us, event | category | flops | bytes accessed | tf_op | source)
XLA Modules:
  0.0 876.8 jit_solution(4694918390599267419)
XLA Ops:
  8.0 13.5 %all-gather.1 = bf16[8,1,128]{2,1,0:T(2,128)(2,1)S(1)} all-gather(bf16[1,1,128]{2,1,0:T(2,128)(2,1)} %bitcast.154), channel_id=1, replica_groups=mesh['rep'=4,'inner'=8] {'inner'}, dimensions={0}, use_global_device_ids=true | all-gather | bytes 2304 | tf_op jit(solution)/shard_map/all_gather | solution.py:59
  24.0 53.2 %all-gather.11.cloned.1.call-done = bf16[1024,3072]{1,0:T(8,128)(2,1)} async-done(((bf16[128,3072]{1,0:T(8,128)(2,1)}), bf16[1024,3072]{1,0:T(8,128)(2,1)}) %all-gather.11.cloned.1.call-update) | async-done | bytes 6291472 | tf_op jit(solution)/shard_map/all_gather | solution.py:55
  77.1 3.9 fusion.70
  85.1 9.2 %all-gather.2 = bf16[8,1,128]{2,1,0:T(2,128)(2,1)S(1)} all-gather(bf16[1,1,128]{2,1,0:T(2,128)(2,1)S(1)} %bitcast.155), channel_id=1, replica_groups=mesh['rep'=4,'inner'=8] {'inner'}, dimensions={0}, use_global_device_ids=true | all-gather | bytes 2304 | tf_op jit(solution)/shard_map/all_gather | solution.py:60
  94.3 17.8 %all-gather.15.cloned.1.call-done = bf16[1024,1024]{0,1:T(8,128)(2,1)} async-done(((bf16[128,1024]{0,1:T(8,128)(2,1)}), bf16[1024,1024]{0,1:T(8,128)(2,1)}) %all-gather.15.cloned.1.call-update) | async-done | bytes 2097168 | tf_op jit(solution)/shard_map/all_gather | solution.py:95
  112.1 4.5 reshape.175
  116.6 2.0 copy.47
  118.6 23.9 %all-gather.13.cloned.1.call-done = bf16[1024,1024]{1,0:T(8,128)(2,1)} async-done(((bf16[128,1024]{1,0:T(8,128)(2,1)}), bf16[1024,1024]{1,0:T(8,128)(2,1)}) %all-gather.13.cloned.1.call-update) | async-done | bytes 2097168 | tf_op jit(solution)/shard_map/all_gather | solution.py:96
  142.5 6.4 reshape.197
  148.9 5.5 copy.46
  154.3 11.6 %while.39 = (s32[]{:T(128)}, f32[16,128]{1,0:T(8,128)S(1)}, f32[16,128]{1,0:T(8,128)S(1)}, bf16[2,512,16,64]{1,3,2,0:T(8,128)(2,1)S(1)}, bf16[128,16,64]{0,2,1:T(8,128)(2,1)S(1)}, /*index=5*/s32[]{:T(128)}, s32[]{:T(128)}) while((s32[]{:T(128)}, f32[16,128]{1,0:T(8,128)S(1)}, f32[16,128]{1,0:T(8,128)S(1)}, ...), condition=%wide.region_5.6_spmd.clone, body=%wide.region_2.5_spmd.clone.sunk | while | flops 139470848 | bytes 9805916 | solution.py:122
  154.3 2.8 bitcast_reduce_fusion.2
  157.2 2.9 fusion.122
  160.2 2.8 bitcast_reduce_fusion.2
  163.0 2.9 fusion.122
  166.0 6.0 while.40
  166.0 2.7 fusion.127
  168.8 2.7 fusion.127
  172.8 2.1 fusion.77
  175.1 100.0 %all-gather.19.cloned.1.call-done = bf16[1024,5248]{1,0:T(8,128)(2,1)} async-done(((bf16[128,5248]{1,0:T(8,128)(2,1)}), bf16[1024,5248]{1,0:T(8,128)(2,1)}) %all-gather.19.cloned.1.call-update) | async-done | bytes 10747920 | tf_op jit(solution)/shard_map/all_gather | solution.py:57
  275.1 7.3 fusion.73
  282.4 49.7 %all-gather.21.cloned.1.call-done = bf16[2624,1024]{1,0:T(8,128)(2,1)} async-done(((bf16[328,1024]{1,0:T(8,128)(2,1)}), bf16[2624,1024]{1,0:T(8,128)(2,1)}) %all-gather.21.cloned.1.call-update) | async-done | bytes 5373968 | tf_op jit(solution)/shard_map/all_gather | solution.py:58
  332.1 7.0 fusion.57
  339.2 1.7 multiply_add_fusion
  340.8 4.4 multiply_reduce_fusion
  345.2 1.4 fusion.74
  348.3 1.5 convolution_convert_fusion.4
  352.1 21.2 %while.41 = (s32[]{:T(128)}, f32[128,16,64]{0,2,1:T(8,128)}, bf16[2,512,16,64]{1,3,2,0:T(8,128)(2,1)}, bf16[2,512,16,64]{1,3,2,0:T(8,128)(2,1)}, bf16[2,512,16,6...) while((s32[]{:T(128)}, f32[128,16,64]{0,2,1:T(8,128)}, ...), condition=%wide.region_14.15_spmd.clone, body=%wide.region_13.14_spmd.clone.sunk | while | flops 680394752 | bytes 87058192 | solution.py:207
  353.6 1.2 copy-done.5
  354.8 1.4 multiply_convert_fusion.6
  356.2 1.8 bitcast_dynamic-update-slice_fusion.4
  358.0 2.7 fusion.139
  360.7 1.9 bitcast_dynamic-update-slice_fusion.5
  364.0 1.2 copy-done.5
  365.2 1.4 multiply_convert_fusion.6
  366.6 1.8 bitcast_dynamic-update-slice_fusion.4
  368.4 2.8 fusion.139
  371.3 1.9 bitcast_dynamic-update-slice_fusion.5
  373.2 6.2 copy.63
  379.5 6.5 reshape.193
  386.0 1.5 copy-done.22
  387.5 4.8 copy.62
  392.3 6.5 reshape.191
  398.9 21.8 %reduce-scatter.21.cloned.1.call-done = bf16[128,1024]{1,0:T(8,128)(2,1)} async-done(((bf16[1024,1024]{1,0:T(8,128)(2,1)}), bf16[128,1024]{1,0:T(8,128)(2,1)}) %reduce-scatter.21.cloned.1.call-update) | async-done | bytes 262160
  422.2 35.3 %reduce-scatter.19.cloned.1.call-done = bf16[128,1024]{1,0:T(8,128)(2,1)} async-done(((bf16[1024,1024]{1,0:T(8,128)(2,1)}), bf16[128,1024]{1,0:T(8,128)(2,1)}) %reduce-scatter.19.cloned.1.call-update) | async-done | bytes 262160
  458.6 4.6 convolution_convert_fusion.2
  464.3 2.0 convolution_convert_fusion.3
  467.4 4.0 convolution_convert_fusion.1
  471.5 1.3 copy-done.9
  472.8 7.3 convolution_convert_fusion
  480.1 51.8 %reduce-scatter.11.cloned.1.call-done = bf16[128,3072]{1,0:T(8,128)(2,1)} async-done(((bf16[1024,3072]{1,0:T(8,128)(2,1)}), bf16[128,3072]{1,0:T(8,128)(2,1)}) %reduce-scatter.11.cloned.1.call-update) | async-done | bytes 786448 | tf_op jit(solution)/shard_map/reduce_scatter | solution.py:238
  532.0 36.8 %reduce-scatter.13.cloned.1.call-done = bf16[128,1024]{1,0:T(8,128)(2,1)} async-done(((bf16[1024,1024]{1,0:T(8,128)(2,1)}), bf16[128,1024]{1,0:T(8,128)(2,1)}) %reduce-scatter.13.cloned.1.call-update) | async-done | bytes 262160 | tf_op jit(solution)/shard_map/reduce_scatter | solution.py:241
  568.9 62.1 %reduce-scatter.17.cloned.1.call-done = bf16[328,1024]{1,0:T(8,128)(2,1)} async-done(((bf16[2624,1024]{1,0:T(8,128)(2,1)}), bf16[328,1024]{1,0:T(8,128)(2,1)}) %reduce-scatter.17.cloned.1.call-update) | async-done | bytes 671760 | tf_op jit(solution)/shard_map/reduce_scatter | solution.py:247
  631.0 112.6 %reduce-scatter.15.cloned.1.call-done = bf16[128,5248]{1,0:T(8,128)(2,1)} async-done(((bf16[1024,5248]{1,0:T(8,128)(2,1)}), bf16[128,5248]{1,0:T(8,128)(2,1)}) %reduce-scatter.15.cloned.1.call-update) | async-done | bytes 1343504 | tf_op jit(solution)/shard_map/reduce_scatter | solution.py:244
  744.9 4.2 fusion.46
  749.1 5.7 fusion.56
  755.1 13.6 %all-reduce.11 = (bf16[1024]{0:T(1024)(128)(2,1)S(1)}, bf16[1024]{0:T(1024)(128)(2,1)S(1)}) all-reduce(bf16[1024]{0:T(1024)(128)(2,1)S(1)} %get-tuple-element.260, bf16[1024]{0:T(1024)(128)(2,1)S(1)} %get-tuple-element.258), channel_id=9, replica_groups=mesh['rep'=4,'inner'=8] {'inner'}, use_global_device_ids=true, to_apply=%region_28.29.clone | all-reduce | flops 2048 | bytes 8192
  768.9 10.0 %all-reduce.12 = (bf16[128]{0:T(256)(128)(2,1)S(1)}, bf16[128]{0:T(256)(128)(2,1)S(1)}) all-reduce(bf16[128]{0:T(256)(128)(2,1)S(1)} %dynamic-slice.1, bf16[128]{0:T(256)(128)(2,1)S(1)} %dynamic-slice.3), channel_id=1, replica_groups=mesh['rep'=4,'inner'=8] {'rep'}, use_global_device_ids=true, to_apply=%region_29.30 | all-reduce | flops 256 | bytes 1024 | tf_op jit(solution)/shard_map/psum | solution.py:262
  780.9 7.3 all-gather.23.cloned.1.call-done
  788.2 2.5 reduce_sum.135
  790.7 1.3 convert_element_type.164
  792.0 72.8 %all-reduce.16.cloned.1.call-done = (bf16[128,1024]{1,0:T(8,128)(2,1)}, bf16[128,5248]{1,0:T(8,128)(2,1)}, bf16[328,1024]{1,0:T(8,128)(2,1)}) async-done(((bf16[128,1024]{1,0:T(8,128)(2,1)}, bf16[128,5248]{1,0:T(8,128)(2,1)}, bf16[328,1024]{1,0:T(8,128)(2,1)}), (bf16[128,1024]{1,0:T(8,128)(2,1)}, bf16[128,5248]{1,0:T(8,128)(2,1)}, bf16[328,1024]{1,0:T(8,128)(2,1)})) %all-reduce.16.cloned.1.call-update) | async-done | bytes 2277392 | tf_op jit(solution)/shard_map/psum | solution.py:259
  864.8 3.1 convert_element_type.168
  867.9 1.2 convert_element_type.170
  (154 shorter events, 23.7 us)
Async XLA Ops:
  7.2 70.0 %copy-start.7 = (bf16[128,1024]{1,0:T(8,128)(2,1)S(1)}, bf16[128,1024]{1,0:T(8,128)(2,1)}, u32[]{:S(2)}) copy-start(bf16[128,1024]{1,0:T(8,128)(2,1)} %param.14) | copy-start | bytes 786436
  7.2 70.0 %all-gather.11.cloned.1.call-start = ((), (), s32[]{:S(2)}) async-start(), calls=%async_computation.6 | async-start | bytes 7077888 | tf_op jit(solution)/shard_map/all_gather | solution.py:55
  7.9 104.2 %all-gather.15.cloned.1.call-start = ((), (), s32[]{:S(2)}) async-start(), calls=%async_computation.8 | async-start | bytes 2359296 | tf_op jit(solution)/shard_map/all_gather | solution.py:95
  82.4 2.7 copy-start.30
  82.4 60.0 %all-gather.13.cloned.1.call-start = ((), (), s32[]{:S(2)}) async-start(), calls=%async_computation.7 | async-start | bytes 2359296 | tf_op jit(solution)/shard_map/all_gather | solution.py:96
  83.3 89.3 %all-gather.17.cloned.1.call-start = ((), (), s32[]{:S(2)}) async-start(), calls=%async_computation.9 | async-start | bytes 2359296 | tf_op jit(solution)/shard_map/all_gather | solution.py:56
  83.8 191.3 %all-gather.19.cloned.1.call-start = ((), (), s32[]{:S(2)}) async-start(), calls=%async_computation.10 | async-start | bytes 12091392 | tf_op jit(solution)/shard_map/all_gather | solution.py:57
  84.4 247.7 %all-gather.21.cloned.1.call-start = ((), (), s32[]{:S(2)}) async-start(), calls=%async_computation.11 | async-start | bytes 6045696 | tf_op jit(solution)/shard_map/all_gather | solution.py:58
  85.0 335.7 %reduce-scatter.21.cloned.1.call-start = ((), (), s32[]{:S(2)}) async-start(), calls=%async_computation.18 | async-start | bytes 2359296
  172.0 0.8 copy-start.23
  172.0 2.9 copy-start.20
  275.1 57.0 %copy-start.16 = (bf16[128,1024]{1,0:T(8,128)(2,1)S(1)}, bf16[128,1024]{1,0:T(8,128)(2,1)}, u32[]{:S(2)}) copy-start(bf16[128,1024]{1,0:T(8,128)(2,1)} %param.15) | copy-start | bytes 786436
  332.1 7.0 copy-start.10
  332.1 8.7 copy-start.4
  339.1 1.7 copy-start.13
  340.8 4.4 copy-start.8
  345.2 3.1 copy-start.12
  346.7 0.8 copy-start.14
  347.6 0.7 copy-start.18
  352.3 1.3 copy-start.2
  352.3 2.5 copy-start.5
  353.6 2.6 copy-start
  358.0 2.7 copy-start.1
  360.7 1.9 copy-start.3
  362.7 1.3 copy-start.2
  362.7 2.5 copy-start.5
  364.0 2.6 copy-start
  368.4 2.8 copy-start.1
  371.3 1.9 copy-start.3
  385.9 1.6 copy-start.22
  386.0 71.5 %reduce-scatter.19.cloned.1.call-start = ((), (), s32[]{:S(2)}) async-start(), calls=%async_computation.17 | async-start | bytes 2359296
  398.8 23.1 %copy-start.6 = (f32[128,16,64]{0,2,1:T(8,128)S(1)}, f32[128,16,64]{0,2,1:T(8,128)}, u32[]{:S(2)}) copy-start(f32[128,16,64]{0,2,1:T(8,128)} %get-tuple-element.127) | copy-start | bytes 1572868
  398.8 133.1 %reduce-scatter.11.cloned.1.call-start = ((), (), s32[]{:S(2)}) async-start(), calls=%async_computation.12 | async-start | bytes 7077888 | tf_op jit(solution)/shard_map/reduce_scatter | solution.py:238
  422.1 41.1 %copy-start.24 = (f32[128,16,64]{0,2,1:T(8,128)}, f32[128,16,64]{0,2,1:T(8,128)S(1)}, u32[]{:S(2)}) copy-start(f32[128,16,64]{0,2,1:T(8,128)S(1)} %get-tuple-element.341) | copy-start | bytes 1572868
  422.2 41.1 %copy-start.26 = (f32[128,16,64]{0,2,1:T(8,128)}, f32[128,16,64]{0,2,1:T(8,128)S(1)}, u32[]{:S(2)}) copy-start(f32[128,16,64]{0,2,1:T(8,128)S(1)} %get-tuple-element.342) | copy-start | bytes 1572868
  463.2 1.0 copy-start.19
  463.2 1.0 copy-start.21
  463.3 105.6 %reduce-scatter.13.cloned.1.call-start = ((), (), s32[]{:S(2)}) async-start(), calls=%async_computation.13 | async-start | bytes 2359296 | tf_op jit(solution)/shard_map/reduce_scatter | solution.py:241
  466.3 1.1 copy-start.11
  466.3 1.2 copy-start.17
  466.3 164.7 %reduce-scatter.17.cloned.1.call-start = ((), (), s32[]{:S(2)}) async-start(), calls=%async_computation.15 | async-start | bytes 6045696 | tf_op jit(solution)/shard_map/reduce_scatter | solution.py:247
  471.4 1.3 copy-start.9
  471.5 272.1 %reduce-scatter.15.cloned.1.call-start = ((), (), s32[]{:S(2)}) async-start(), calls=%async_computation.14 | async-start | bytes 12091392 | tf_op jit(solution)/shard_map/reduce_scatter | solution.py:244
  480.1 263.5 %copy-start.31 = (u32[32]{0:T(128)S(1)}, u32[32]{0:T(128)}, u32[]{:S(2)}) copy-start(u32[32]{0:T(128)} %constant.154) | copy-start | bytes 388
  480.1 308.1 %all-gather.23.cloned.1.call-start = ((), (), s32[]{:S(2)}) async-start(), calls=%async_computation.16 | async-start | bytes 3932160 | tf_op jit(solution)/shard_map/all_gather | solution.py:258
  532.0 332.9 %all-reduce.16.cloned.1.call-start = ((), (), s32[]{:S(2)}) async-start(), calls=%async_computation.19 | async-start | bytes 4554752 | tf_op jit(solution)/shard_map/psum | solution.py:259
  744.8 4.3 copy-start.25
  744.8 4.2 copy-start.27
  749.1 30.8 %copy-start.15 = (f32[128,1024]{1,0:T(8,128)S(1)}, f32[128,1024]{1,0:T(8,128)}, u32[]{:S(2)}) copy-start(f32[128,1024]{1,0:T(8,128)} %copy-done.14) | copy-start | bytes 1572868
  864.8 3.1 copy-start.28
  867.9 1.2 copy-start.29
Sparse Core Ops, SparseCore 0:
  9.7 67.4 all-gather.10
  82.5 29.4 all-gather.14
  114.3 28.1 all-gather.12
  143.9 28.5 all-gather.16
  174.0 101.0 all-gather.18
  276.6 55.4 all-gather.20
  386.1 34.5 reduce-scatter.20
  423.0 34.4 reduce-scatter.18
  463.4 68.5 reduce-scatter.10
  534.7 34.1 reduce-scatter.12
  571.2 59.7 reduce-scatter.16
  633.3 110.2 reduce-scatter.14
  745.5 42.5 all-gather.22
  791.9 72.9 all-reduce.15
